TPU v7x, 32 devices: a whole 2x2x4 slice. The times are simulated.
32 devices in a mesh: groups: 2 (over y), expert: 4 (over z), dp: 4 (over x, core).
Axes of the slice: x: 2, y: 2, z: 4, core: 2. Of those that a mesh axis runs over, the one named last changes fastest.
Arguments:
- tokens: bfloat16 [2048, 1024], P(('groups', 'expert', 'dp')), parts along dimension 0, may hold values from -6 to 6
- expert_ids: int32 [2048, 8], P(('groups', 'expert', 'dp')), parts along dimension 0, may hold values from 0 to 31, all different within a row; in each aligned block of 64 rows (0 to 63, 64 to 127, ...) at most 32 rows name the same one
- route_scores: float32 [2048, 8], P(('groups', 'expert', 'dp')), parts along dimension 0, may hold values from 0.05 to 1
- w_gate: bfloat16 [32, 1024, 768], P('expert'), may hold values from -0.1875 to 0.1875
- w_up: bfloat16 [32, 1024, 768], P('expert'), may hold values from -0.1875 to 0.1875
- w_down: bfloat16 [32, 768, 1024], P('expert'), may hold values from -0.21875 to 0.21875
Outputs:
- mixed: bfloat16 [2048, 1024], P(('groups', 'expert', 'dp')), parts along dimension 0
There are 2 independent parts, one for each index of `groups`. A program takes and returns all parts, laid end to end along the dimension named above; an argument that names none is the same for every part. Nothing has to cross between parts.
Inputs may be any that keep to these rules, and one draw needn't show every extreme that they name: `expert_ids`: within the 64 rows of one device no expert is named by more than 32 rows, and in every draw some expert is named by exactly 32 rows of some device.
All inputs are finite; a program needn't handle non-finite values.
Results may differ from a plain program's by a relative error of at most 0.0064.
Values may be sent and summed in bfloat16 or wider, within the bound.
No kernel may reach another device: no remote copies, remote signals or barrier semaphores. Data moves between devices by JAX's collectives and lax.ppermute only.
A program may use at most 128 MiB of HBM per device.

v0:
```python
import math
import jax
import jax.numpy as jnp
from jax import lax
from jax.sharding import PartitionSpec as P

EXPERTS = 32
TOP = 8
CAP = 32


def lookup(values, indices, length):
    match = indices[:, None] == jnp.arange(length, dtype=jnp.int32)[None, :]
    return jnp.sum(jnp.where(match, values[None, :], 0), axis=1)


def compact_plan(source_counts, peer_count):
    slot_span = peer_count * CAP
    source_ends = jnp.cumsum(source_counts)
    starts = source_ends - source_counts
    position = jnp.arange(slot_span, dtype=jnp.int32)
    source_of = jnp.minimum(
        jnp.sum((source_ends[None, :] <= position[:, None]).astype(jnp.int32), axis=1),
        peer_count - 1,
    )
    gather_at = jnp.clip(
        source_of * CAP + position - lookup(starts, source_of, peer_count), 0, slot_span - 1
    )
    live_rows = position < source_ends[peer_count - 1]
    return (gather_at, live_rows, starts)


def spread_back(compact_out, source_counts, starts, peer_count):
    slot_span = peer_count * CAP
    position = jnp.arange(slot_span, dtype=jnp.int32)
    source_of = position // CAP
    within = position % CAP
    from_pos = jnp.minimum(lookup(starts, source_of, peer_count) + within, slot_span - 1)
    live_slots = within < lookup(source_counts, source_of, peer_count)
    return jnp.where(live_slots[:, None], compact_out[from_pos], jnp.zeros((), jnp.bfloat16))


def expert_rows(row_block, scale_block, weight_set, row_count, tile_rows):
    gate_matrix, up_matrix, down_matrix = weight_set
    initial = jnp.zeros(row_block.shape, jnp.bfloat16)
    turn_count = (row_count + tile_rows - 1) // tile_rows

    def advance(loop_state):
        turn_index, filled = loop_state
        offset = turn_index * tile_rows
        part_rows = lax.dynamic_slice_in_dim(row_block, offset, tile_rows, 0)
        part_scale = lax.dynamic_slice_in_dim(scale_block, offset, tile_rows, 0)
        gate_values = jnp.dot(part_rows, gate_matrix, preferred_element_type=jnp.float32)
        up_values = jnp.dot(part_rows, up_matrix, preferred_element_type=jnp.float32)
        hidden = (jax.nn.silu(gate_values) * up_values).astype(jnp.bfloat16)
        projected = jnp.dot(hidden, down_matrix, preferred_element_type=jnp.float32)
        scaled = (part_scale.astype(jnp.float32)[:, None] * projected).astype(jnp.bfloat16)
        return (turn_index + 1, lax.dynamic_update_slice_in_dim(filled, scaled, offset, 0))

    def pending(loop_state):
        return loop_state[0] < turn_count

    return lax.while_loop(pending, advance, (jnp.int32(0), initial))[1]


def per_device(tokens, expert_ids, route_scores, w_gate, w_up, w_down):
    peer_count = lax.axis_size("expert")
    local_experts = w_gate.shape[0]
    token_count = tokens.shape[0]
    model_width = tokens.shape[1]
    slot_count = token_count * TOP
    slot_span = peer_count * CAP
    half_span = slot_span // 2
    tile_rows = math.gcd(half_span, 256)
    route_weights = (route_scores / jnp.sum(route_scores, axis=1, keepdims=True)).astype(
        jnp.bfloat16
    )
    flat_ids = expert_ids.reshape(slot_count)
    onehot = (flat_ids[:, None] == jnp.arange(EXPERTS, dtype=jnp.int32)[None, :]).astype(jnp.int32)
    slot_ranks = jnp.sum((jnp.cumsum(onehot, axis=0) - 1) * onehot, axis=1)
    targets = flat_ids * CAP + slot_ranks
    source_slot = (
        jnp.full((EXPERTS * CAP,), slot_count, jnp.int32)
        .at[targets]
        .set(jnp.arange(slot_count, dtype=jnp.int32))
    )
    padded_tokens = jnp.concatenate([tokens, jnp.zeros((1, model_width), jnp.bfloat16)], axis=0)
    padded_weights = jnp.concatenate(
        [route_weights.reshape(slot_count), jnp.zeros((1,), jnp.bfloat16)]
    )
    send_rows = padded_tokens[source_slot // TOP].reshape(EXPERTS, CAP, model_width)
    send_scale = padded_weights[source_slot].reshape(EXPERTS, CAP)
    recv_rows, recv_scale = (
        lax.all_to_all(send_rows, "expert", split_axis=0, concat_axis=1, tiled=True),
        lax.all_to_all(send_scale, "expert", split_axis=0, concat_axis=1, tiled=True),
    )
    compact_rows = []
    compact_scale = []
    count_list = []
    start_list = []
    total_list = []
    for member in range(local_experts):
        source_counts = jnp.sum(
            (recv_scale[member].reshape(peer_count, CAP) > 0).astype(jnp.int32), axis=1
        )
        gather_at, live_rows, starts = compact_plan(source_counts, peer_count)
        compact_rows.append(
            jnp.where(live_rows[:, None], recv_rows[member][gather_at], jnp.zeros((), jnp.bfloat16))
        )
        compact_scale.append(
            jnp.where(live_rows, recv_scale[member][gather_at], jnp.zeros((), jnp.bfloat16))
        )
        count_list.append(source_counts)
        start_list.append(starts)
        total_list.append(jnp.sum(source_counts))
    results = []
    for member in range(local_experts):
        results.append(
            expert_rows(
                compact_rows[member],
                compact_scale[member],
                (w_gate[member], w_up[member], w_down[member]),
                total_list[member],
                tile_rows,
            )
        )
    slot_results = jnp.stack(
        [
            spread_back(results[member], count_list[member], start_list[member], peer_count)
            for member in range(local_experts)
        ]
    )
    returned = lax.all_to_all(slot_results, "expert", split_axis=1, concat_axis=0, tiled=True)
    returned_flat = returned.reshape(EXPERTS * CAP, model_width)
    picked = returned_flat[targets].astype(jnp.float32).reshape(token_count, TOP, model_width)
    return jnp.sum(picked, axis=1).astype(jnp.bfloat16)


def solution(mesh):
    placed = (
        P(("groups", "expert", "dp"), None),
        P(("groups", "expert", "dp"), None),
        P(("groups", "expert", "dp"), None),
        P("expert", None, None),
        P("expert", None, None),
        P("expert", None, None),
    )
    return jax.shard_map(
        per_device,
        mesh=mesh,
        in_specs=placed,
        out_specs=P(("groups", "expert", "dp"), None),
        check_vma=False,
    )
```

profile of v0, /device:TPU:0, one launch (start us, length us, event | category | flops | bytes accessed | tf_op | source)
XLA Modules:
  0.0 296.0 jit_solution(2162845717473998222)
XLA Ops:
  5.0 2.4 scatter_custom_fusion
  7.5 6.8 %gather_fusion = bf16[1024]{0:T(1024)(128)(2,1)S(1)} fusion(bf16[513]{0:T(1024)(128)(2,1)S(1)} %pad_maximum_fusion, s32[1024]{0:T(1024)S(1)} %get-tuple-element.566), kind=kCustom, calls=%fused_computation | custom fusion | bytes 8192 | tf_op jit(solution)/shard_map/gather | solution.py:92
  15.1 6.3 %all-to-all-start = ((bf16[4,2,128]{2,1,0:T(2,128)(2,1)}), bf16[4,2,128]{2,1,0:T(2,128)(2,1)S(1)}, u32[]{:S(2)}, u32[]{:S(2)}) async-start(bf16[4,2,128]{2,1,0:T(2,128)(2,1)} %reshape.1325), calls=%async_computation | async-start | bytes 4096 | tf_op jit(solution)/shard_map/all_to_all | solution.py:95
  21.4 9.6 %slice_bitcast_fusion = (bf16[768,1024]{1,0:T(8,128)(2,1)}, bf16[768,1024]{1,0:T(8,128)(2,1)}, bf16[768,1024]{1,0:T(8,128)(2,1)}, bf16[768,1024]{1,0:T(8,128)(2,...) fusion(bf16[8,768,1024]{2,1,0:T(8,128)(2,1)} %param.27), kind=kLoop, calls=%fused_computation.173 | loop fusion | bytes 25165824 | tf_op jit(solution)/shard_map/squeeze | solution.py:122
  31.0 17.0 %slice_bitcast_fusion.1 = (bf16[1024,768]{1,0:T(8,128)(2,1)S(1)}, bf16[1024,768]{1,0:T(8,128)(2,1)}, bf16[1024,768]{1,0:T(8,128)(2,1)}, bf16[1024,768]{1,0:T(8,1...) fusion(bf16[8,1024,768]{2,1,0:T(8,128)(2,1)} %param.26, ...), kind=kLoop, calls=%fused_computation.174 | loop fusion | bytes 50331648 | tf_op jit(solution)/shard_map/squeeze | solution.py:122
  48.1 5.4 %gather_fusion.2 = bf16[1024,1024]{1,0:T(8,128)(2,1)} fusion(bf16[65,1024]{1,0:T(8,128)(2,1)S(1)} %concatenate.7, s32[1024]{0:T(1024)S(1)} %get-tuple-element.565), kind=kCustom, calls=%fused_computation.2 | custom fusion | bytes 4198400 | tf_op jit(solution)/shard_map/gather | solution.py:91
  53.5 5.1 %all-to-all-start.1 = ((bf16[32,32,1024]{2,1,0:T(8,128)(2,1)}), bf16[32,32,1024]{2,1,0:T(8,128)(2,1)}, u32[]{:S(2)}, u32[]{:S(2)}) async-start(bf16[32,32,1024]{2,1,0:T(8,128)(2,1)} %bitcast.390), calls=%async_computation.1 | async-start | bytes 4194304 | tf_op jit(solution)/shard_map/all_to_all | solution.py:94
  58.7 1.4 fusion.168
  96.4 9.9 %all-to-all-done.1 = bf16[32,32,1024]{2,1,0:T(8,128)(2,1)} async-done(((bf16[32,32,1024]{2,1,0:T(8,128)(2,1)}), bf16[32,32,1024]{2,1,0:T(8,128)(2,1)}, u32[]{:S(2)}, u32[]{:S(2)}) %all-to-all-start.1) | async-done | bytes 2097184 | tf_op jit(solution)/shard_map/all_to_all | solution.py:94
  106.3 1.8 copy.42
  109.4 2.7 gather_fusion.3
  112.1 1.7 broadcast_select_fusion.7
  114.6 12.2 %while.80 = (s32[]{:T(128)}, bf16[128,1024]{1,0:T(8,128)(2,1)}, s32[]{:T(128)}, bf16[128]{0:T(256)(128)(2,1)S(1)}, bf16[128,1024]{1,0:T(8,128)(2,1)}, /*index=5*...) while((s32[]{:T(128)}, bf16[128,1024]{1,0:T(8,128)(2,1)}, ...), condition=%wide.region_12.13_spmd, body=%wide.region_11.12_spmd.sunk | while | flops 302415936 | bytes 5506867 | solution.py:63
  114.6 2.6 fusion.295
  117.2 3.4 %fusion.296 = bf16[128,1024]{1,0:T(8,128)(2,1)} fusion(bf16[128,1024]{1,0:T(8,128)(2,1)} %get-tuple-element.989, s32[]{:T(128)S(6)} %select_n.860, bf16[768,1024]{1,0:T(8,128)(2,1)} %get-tuple-element.1007, bf16[1024,768]{1,0:T(8,128)(2,1)} %get-tuple-element.1006, f32[64,768]{1,0:T(8,128)} %fusion.295, f32[64]{0:T(128)S(1)} %dynamic-slice_convert_fusion.16, ...), kind=kOutput, calls=%fused_computation.31.clone.1 | convolution fusion | flops 201752576 | bytes 3605760 | tf_op jit(solution)/shard_map/while/body/dot_general | solution.py:56
  120.7 2.6 fusion.295
  123.3 3.4 %fusion.296 = bf16[128,1024]{1,0:T(8,128)(2,1)} fusion(bf16[128,1024]{1,0:T(8,128)(2,1)} %get-tuple-element.989, s32[]{:T(128)S(6)} %select_n.860, bf16[768,1024]{1,0:T(8,128)(2,1)} %get-tuple-element.1007, bf16[1024,768]{1,0:T(8,128)(2,1)} %get-tuple-element.1006, f32[64,768]{1,0:T(8,128)} %fusion.295, f32[64]{0:T(128)S(1)} %dynamic-slice_convert_fusion.16, ...), kind=kOutput, calls=%fused_computation.31.clone.1 | convolution fusion | flops 201752576 | bytes 3605760 | tf_op jit(solution)/shard_map/while/body/dot_general | solution.py:56
  126.8 2.7 gather_fusion.6
  129.5 1.7 broadcast_select_fusion.6
  132.0 6.1 %while.81 = (s32[]{:T(128)}, bf16[128,1024]{1,0:T(8,128)(2,1)}, s32[]{:T(128)}, bf16[128]{0:T(256)(128)(2,1)S(1)}, bf16[128,1024]{1,0:T(8,128)(2,1)}, /*index=5*...) while((s32[]{:T(128)}, bf16[128,1024]{1,0:T(8,128)(2,1)}, ...), condition=%wide.region_21.22_spmd, body=%wide.region_20.21_spmd.sunk | while | flops 302415936 | bytes 5506867 | solution.py:63
  132.0 2.6 fusion.302
  134.7 3.5 %fusion.303 = bf16[128,1024]{1,0:T(8,128)(2,1)} fusion(bf16[128,1024]{1,0:T(8,128)(2,1)} %get-tuple-element.1025, s32[]{:T(128)S(6)} %select_n.861, bf16[768,1024]{1,0:T(8,128)(2,1)} %get-tuple-element.1043, bf16[1024,768]{1,0:T(8,128)(2,1)} %get-tuple-element.1042, f32[64,768]{1,0:T(8,128)} %fusion.302, f32[64]{0:T(128)S(1)} %dynamic-slice_convert_fusion.17, ...), kind=kOutput, calls=%fused_computation.49.clone.1 | convolution fusion | flops 201752576 | bytes 3605760 | tf_op jit(solution)/shard_map/while/body/dot_general | solution.py:56
  138.1 2.7 gather_fusion.9
  140.8 1.8 broadcast_select_fusion.5
  143.3 6.1 %while.82 = (s32[]{:T(128)}, bf16[128,1024]{1,0:T(8,128)(2,1)}, s32[]{:T(128)}, bf16[128]{0:T(256)(128)(2,1)S(1)}, bf16[128,1024]{1,0:T(8,128)(2,1)}, /*index=5*...) while((s32[]{:T(128)}, bf16[128,1024]{1,0:T(8,128)(2,1)}, ...), condition=%wide.region_30.31_spmd, body=%wide.region_29.30_spmd.sunk | while | flops 302415936 | bytes 5506867 | solution.py:63
  143.3 2.6 fusion.309
  146.0 3.4 %fusion.310 = bf16[128,1024]{1,0:T(8,128)(2,1)} fusion(bf16[128,1024]{1,0:T(8,128)(2,1)} %get-tuple-element.1061, s32[]{:T(128)S(6)} %select_n.862, bf16[768,1024]{1,0:T(8,128)(2,1)} %get-tuple-element.1079, bf16[1024,768]{1,0:T(8,128)(2,1)} %get-tuple-element.1078, f32[64,768]{1,0:T(8,128)} %fusion.309, f32[64]{0:T(128)S(1)} %dynamic-slice_convert_fusion.18, ...), kind=kOutput, calls=%fused_computation.67.clone.1 | convolution fusion | flops 201752576 | bytes 3605760 | tf_op jit(solution)/shard_map/while/body/dot_general | solution.py:56
  149.4 2.7 gather_fusion.12
  152.2 1.8 broadcast_select_fusion.4
  154.6 12.1 %while.83 = (s32[]{:T(128)}, bf16[128,1024]{1,0:T(8,128)(2,1)}, s32[]{:T(128)}, bf16[128]{0:T(256)(128)(2,1)S(1)}, bf16[128,1024]{1,0:T(8,128)(2,1)}, /*index=5*...) while((s32[]{:T(128)}, bf16[128,1024]{1,0:T(8,128)(2,1)}, ...), condition=%wide.region_39.40_spmd, body=%wide.region_38.39_spmd.sunk | while | flops 302415936 | bytes 5506867 | solution.py:63
  154.6 2.5 fusion.316
  157.3 3.4 %fusion.317 = bf16[128,1024]{1,0:T(8,128)(2,1)} fusion(bf16[128,1024]{1,0:T(8,128)(2,1)} %get-tuple-element.1097, s32[]{:T(128)S(6)} %select_n.863, bf16[768,1024]{1,0:T(8,128)(2,1)} %get-tuple-element.1115, bf16[1024,768]{1,0:T(8,128)(2,1)} %get-tuple-element.1114, f32[64,768]{1,0:T(8,128)} %fusion.316, f32[64]{0:T(128)S(1)} %dynamic-slice_convert_fusion.19, ...), kind=kOutput, calls=%fused_computation.85.clone.1 | convolution fusion | flops 201752576 | bytes 3605760 | tf_op jit(solution)/shard_map/while/body/dot_general | solution.py:56
  160.7 2.5 fusion.316
  163.3 3.5 %fusion.317 = bf16[128,1024]{1,0:T(8,128)(2,1)} fusion(bf16[128,1024]{1,0:T(8,128)(2,1)} %get-tuple-element.1097, s32[]{:T(128)S(6)} %select_n.863, bf16[768,1024]{1,0:T(8,128)(2,1)} %get-tuple-element.1115, bf16[1024,768]{1,0:T(8,128)(2,1)} %get-tuple-element.1114, f32[64,768]{1,0:T(8,128)} %fusion.316, f32[64]{0:T(128)S(1)} %dynamic-slice_convert_fusion.19, ...), kind=kOutput, calls=%fused_computation.85.clone.1 | convolution fusion | flops 201752576 | bytes 3605760 | tf_op jit(solution)/shard_map/while/body/dot_general | solution.py:56
  166.8 2.7 gather_fusion.15
  169.5 1.8 broadcast_select_fusion.3
  172.0 6.1 %while.84 = (s32[]{:T(128)}, bf16[128,1024]{1,0:T(8,128)(2,1)}, s32[]{:T(128)}, bf16[128]{0:T(256)(128)(2,1)S(1)}, bf16[128,1024]{1,0:T(8,128)(2,1)}, /*index=5*...) while((s32[]{:T(128)}, bf16[128,1024]{1,0:T(8,128)(2,1)}, ...), condition=%wide.region_48.49_spmd, body=%wide.region_47.48_spmd.sunk | while | flops 302415936 | bytes 5506867 | solution.py:63
  172.0 2.5 fusion.323
  174.6 3.4 %fusion.324 = bf16[128,1024]{1,0:T(8,128)(2,1)} fusion(bf16[128,1024]{1,0:T(8,128)(2,1)} %get-tuple-element.1133, s32[]{:T(128)S(6)} %select_n.864, bf16[768,1024]{1,0:T(8,128)(2,1)} %get-tuple-element.1151, bf16[1024,768]{1,0:T(8,128)(2,1)} %get-tuple-element.1150, f32[64,768]{1,0:T(8,128)} %fusion.323, f32[64]{0:T(128)S(1)} %dynamic-slice_convert_fusion.20, ...), kind=kOutput, calls=%fused_computation.103.clone.1 | convolution fusion | flops 201752576 | bytes 3605760 | tf_op jit(solution)/shard_map/while/body/dot_general | solution.py:56
  178.1 2.7 gather_fusion.18
  180.8 1.7 broadcast_select_fusion.2
  183.3 12.2 %while.85 = (s32[]{:T(128)}, bf16[128,1024]{1,0:T(8,128)(2,1)}, s32[]{:T(128)}, bf16[128]{0:T(256)(128)(2,1)S(1)}, bf16[128,1024]{1,0:T(8,128)(2,1)}, /*index=5*...) while((s32[]{:T(128)}, bf16[128,1024]{1,0:T(8,128)(2,1)}, ...), condition=%wide.region_57.58_spmd, body=%wide.region_56.57_spmd.sunk | while | flops 302415936 | bytes 5506867 | solution.py:63
  183.3 2.6 fusion.330
  186.0 3.4 %fusion.331 = bf16[128,1024]{1,0:T(8,128)(2,1)} fusion(bf16[128,1024]{1,0:T(8,128)(2,1)} %get-tuple-element.1169, s32[]{:T(128)S(6)} %select_n.865, bf16[768,1024]{1,0:T(8,128)(2,1)} %get-tuple-element.1187, bf16[1024,768]{1,0:T(8,128)(2,1)} %get-tuple-element.1186, f32[64,768]{1,0:T(8,128)} %fusion.330, f32[64]{0:T(128)S(1)} %dynamic-slice_convert_fusion.21, ...), kind=kOutput, calls=%fused_computation.121.clone.1 | convolution fusion | flops 201752576 | bytes 3605760 | tf_op jit(solution)/shard_map/while/body/dot_general | solution.py:56
  189.4 2.6 fusion.330
  192.0 3.4 %fusion.331 = bf16[128,1024]{1,0:T(8,128)(2,1)} fusion(bf16[128,1024]{1,0:T(8,128)(2,1)} %get-tuple-element.1169, s32[]{:T(128)S(6)} %select_n.865, bf16[768,1024]{1,0:T(8,128)(2,1)} %get-tuple-element.1187, bf16[1024,768]{1,0:T(8,128)(2,1)} %get-tuple-element.1186, f32[64,768]{1,0:T(8,128)} %fusion.330, f32[64]{0:T(128)S(1)} %dynamic-slice_convert_fusion.21, ...), kind=kOutput, calls=%fused_computation.121.clone.1 | convolution fusion | flops 201752576 | bytes 3605760 | tf_op jit(solution)/shard_map/while/body/dot_general | solution.py:56
  195.5 2.7 gather_fusion.21
  198.2 1.7 broadcast_select_fusion.1
  200.7 11.4 %while.86 = (s32[]{:T(128)}, bf16[128,1024]{1,0:T(8,128)(2,1)}, s32[]{:T(128)}, bf16[128]{0:T(256)(128)(2,1)S(1)}, bf16[128,1024]{1,0:T(8,128)(2,1)}, /*index=5*...) while((s32[]{:T(128)}, bf16[128,1024]{1,0:T(8,128)(2,1)}, ...), condition=%wide.region_66.67_spmd, body=%wide.region_65.66_spmd.sunk | while | flops 302415936 | bytes 5506867 | solution.py:63
  200.7 2.6 fusion.337
  203.4 3.1 %fusion.338 = bf16[128,1024]{1,0:T(8,128)(2,1)} fusion(bf16[128,1024]{1,0:T(8,128)(2,1)} %get-tuple-element.1205, s32[]{:T(128)S(6)} %select_n.866, bf16[768,1024]{1,0:T(8,128)(2,1)} %get-tuple-element.1223, bf16[1024,768]{1,0:T(8,128)(2,1)S(1)} %get-tuple-element.1222, f32[64,768]{1,0:T(8,128)} %fusion.337, ...), kind=kOutput, calls=%fused_computation.139.clone.1 | convolution fusion | flops 201752576 | bytes 3605760 | tf_op jit(solution)/shard_map/while/body/dot_general | solution.py:56
  206.4 2.6 fusion.337
  209.1 3.1 %fusion.338 = bf16[128,1024]{1,0:T(8,128)(2,1)} fusion(bf16[128,1024]{1,0:T(8,128)(2,1)} %get-tuple-element.1205, s32[]{:T(128)S(6)} %select_n.866, bf16[768,1024]{1,0:T(8,128)(2,1)} %get-tuple-element.1223, bf16[1024,768]{1,0:T(8,128)(2,1)S(1)} %get-tuple-element.1222, f32[64,768]{1,0:T(8,128)} %fusion.337, ...), kind=kOutput, calls=%fused_computation.139.clone.1 | convolution fusion | flops 201752576 | bytes 3605760 | tf_op jit(solution)/shard_map/while/body/dot_general | solution.py:56
  212.1 1.6 gather_fusion.24
  213.7 1.7 broadcast_select_fusion
  215.5 9.2 %while.87 = (s32[]{:T(128)}, bf16[128,1024]{1,0:T(8,128)(2,1)S(1)}, s32[]{:T(128)}, bf16[128]{0:T(256)(128)(2,1)S(1)}, bf16[128,1024]{1,0:T(8,128)(2,1)}, /*inde...) while((s32[]{:T(128)}, bf16[128,1024]{1,0:T(8,128)(2,1)S(1)}, ...), condition=%wide.region_75.76_spmd, body=%wide.region_74.75_spmd.sunk | while | flops 302415936 | bytes 5507123 | solution.py:63
  215.5 2.0 fusion.344
  217.6 2.4 fusion.345
  220.0 2.0 fusion.344
  222.0 2.4 fusion.345
  224.7 2.1 gather_fusion.4
  239.6 2.7 copy.37
  242.4 49.1 %all_to_all.46 = bf16[8,128,1024]{2,0,1:T(8,128)(2,1)S(1)} all-to-all(bf16[8,128,1024]{2,0,1:T(8,128)(2,1)S(1)} %copy.37), channel_id=1, replica_groups=mesh['groups'=2,'expert'=4,'dp'=4] {'expert'}, dimensions={1} | all-to-all | bytes 4194304 | tf_op jit(solution)/shard_map/all_to_all | solution.py:133
  292.6 2.1 gather_fusion.26
  (206 shorter events, 59.2 us)
Async XLA Ops:
  15.1 38.4 %all-to-all-start = ((bf16[4,2,128]{2,1,0:T(2,128)(2,1)}), bf16[4,2,128]{2,1,0:T(2,128)(2,1)S(1)}, u32[]{:S(2)}, u32[]{:S(2)}) async-start(bf16[4,2,128]{2,1,0:T(2,128)(2,1)} %reshape.1325), calls=%async_computation | async-start | bytes 4096 | tf_op jit(solution)/shard_map/all_to_all | solution.py:95
  31.0 17.1 %copy-start.7 = (bf16[64,1024]{1,0:T(8,128)(2,1)S(1)}, bf16[64,1024]{1,0:T(8,128)(2,1)}, u32[]{:S(2)}) copy-start(bf16[64,1024]{1,0:T(8,128)(2,1)} %param.22) | copy-start | bytes 393220
  53.5 52.8 %all-to-all-start.1 = ((bf16[32,32,1024]{2,1,0:T(8,128)(2,1)}), bf16[32,32,1024]{2,1,0:T(8,128)(2,1)}, u32[]{:S(2)}, u32[]{:S(2)}) async-start(bf16[32,32,1024]{2,1,0:T(8,128)(2,1)} %bitcast.390), calls=%async_computation.1 | async-start | bytes 4194304 | tf_op jit(solution)/shard_map/all_to_all | solution.py:94
  126.8 5.2 %copy-start.12 = (bf16[128]{0:T(256)(128)(2,1)S(1)}, bf16[128]{0:T(256)(128)(2,1)}, u32[]{:S(2)}) copy-start(bf16[128]{0:T(256)(128)(2,1)} %broadcast_select_fusion.14) | copy-start | bytes 772
  138.1 5.2 %copy-start.11 = (bf16[128]{0:T(256)(128)(2,1)S(1)}, bf16[128]{0:T(256)(128)(2,1)}, u32[]{:S(2)}) copy-start(bf16[128]{0:T(256)(128)(2,1)} %broadcast_select_fusion.13) | copy-start | bytes 772
  149.4 5.2 %copy-start.10 = (bf16[128]{0:T(256)(128)(2,1)S(1)}, bf16[128]{0:T(256)(128)(2,1)}, u32[]{:S(2)}) copy-start(bf16[128]{0:T(256)(128)(2,1)} %broadcast_select_fusion.12) | copy-start | bytes 772
  166.8 5.2 %copy-start.9 = (bf16[128]{0:T(256)(128)(2,1)S(1)}, bf16[128]{0:T(256)(128)(2,1)}, u32[]{:S(2)}) copy-start(bf16[128]{0:T(256)(128)(2,1)} %broadcast_select_fusion.11) | copy-start | bytes 772
  178.1 5.2 %copy-start.8 = (bf16[128]{0:T(256)(128)(2,1)S(1)}, bf16[128]{0:T(256)(128)(2,1)}, u32[]{:S(2)}) copy-start(bf16[128]{0:T(256)(128)(2,1)} %broadcast_select_fusion.10) | copy-start | bytes 772
  212.1 3.4 %copy-start = (bf16[1024,768]{1,0:T(8,128)(2,1)S(1)}, bf16[1024,768]{1,0:T(8,128)(2,1)}, u32[]{:S(2)}) copy-start(bf16[1024,768]{1,0:T(8,128)(2,1)} %get-tuple-element.1233) | copy-start | bytes 4718596
  224.7 2.9 copy-start.1
  226.8 1.7 copy-start.2
  228.4 1.0 copy-start.3
  229.3 1.0 copy-start.4
  230.3 1.0 copy-start.5
  231.2 1.0 copy-start.6
where the time goes:
time: 298 us; the launch traced here: 296 us
  local copies, waits for them, and re-layouts  102 us (34%)
  matrix products  74 us (25%)
  blocking collectives  49.1 us (16%)
  other arithmetic  42.9 us (14%)
  starting transfers between devices  11.4 us (4%)
  waiting for transfers between devices  9.93 us (3%)
  between operations  5.99 us (2%)
    all_to_all x1, blocking collectives, per_device(): lax.all_to_all(slot_results, 'expert', split_axis=1, concat_axis=0, tiled...  49.1 us
    dot_general x13, matrix products, advance(): projected = jnp.dot(hidden, down_matrix, preferred_element_type=jnp.float32)  41.9 us
    dot_general x13, matrix products, advance(): jnp.dot(part_rows, gate_matrix, preferred_element_type=jnp.float32)  32.1 us
    gather x8, local copies, waits for them, and re-layouts, per_device(): recv_rows[member][gather_at]  20.7 us
    squeeze x1, local copies, waits for them, and re-layouts, per_device(): w_up[member]  17 us
    select_n x8, other arithmetic, per_device(): jnp.where(live_rows[:, None], recv_rows[member][gather_at], jnp.zeros((),...  14 us
    all_to_all x1, waiting for transfers between devices, per_device(): lax.all_to_all(send_rows, 'expert', split_axis=0, concat_axis=1, tiled=True)  9.93 us
    gather x8, local copies, waits for them, and re-layouts, per_device(): recv_scale[member][gather_at]  9.85 us
  transfers between devices with their start and end apart: 2, of which 1 were waited for; matrix products, arithmetic and copies ran while one was open for 22% of the time, Pallas kernels for 0%

commit v1 on v0

--- a/solution.py
+++ b/solution.py
@@ -7,6 +7,17 @@
 EXPERTS = 32
 TOP = 8
 CAP = 32
+
+
+def split_up(shard, dim, size):
+    before, after = (shard.shape[:dim], shard.shape[dim + 1 :])
+    return jnp.moveaxis(shard.reshape(*before, size, -1, *after), dim, 0)
+
+
+def laid_out(blocks, dim):
+    shape = list(blocks.shape[1:])
+    shape[dim] *= blocks.shape[0]
+    return jnp.moveaxis(blocks, 0, dim).reshape(shape)
 
 
 def lookup(values, indices, length):
@@ -130,7 +141,14 @@
             for member in range(local_experts)
         ]
     )
-    returned = lax.all_to_all(slot_results, "expert", split_axis=1, concat_axis=0, tiled=True)
+    size, index = (lax.axis_size("expert"), lax.axis_index("expert"))
+    parts = split_up(slot_results, 1, size)
+    outs = [parts[index]]
+    for lap in range(1, size):
+        sent = parts[index ^ lap]
+        outs.append(lax.ppermute(sent, "expert", [(i, i ^ lap) for i in range(size)]))
+    parts = jnp.stack(outs)[index ^ jnp.arange(size)]
+    returned = laid_out(parts, 0)
     returned_flat = returned.reshape(EXPERTS * CAP, model_width)
     picked = returned_flat[targets].astype(jnp.float32).reshape(token_count, TOP, model_width)
     return jnp.sum(picked, axis=1).astype(jnp.bfloat16)

time: 298 us -> 284 us (0.953)
  blocking collectives: 49.1 us -> 0 us
  waiting for transfers between devices: 9.93 us -> 38.6 us
  starting transfers between devices: 11.4 us -> 15.9 us
  local copies, waits for them, and re-layouts: 102 us -> 106 us
  other arithmetic: 42.9 us -> 39.2 us
    all_to_all x1 -> x0, blocking collectives: 49.1 us -> none  [per_device(): lax.all_to_all(slot_results, 'expert', split_axis=1, concat_axis=0, tiled...]
    ppermute x0 -> x3, waiting for transfers between devices: none -> 29.8 us  [per_device(): lax.ppermute(sent, 'expert', [(i, i ^ lap) for i in range(size)])]
    unnamed x7, other arithmetic: 5.75 us -> 0.8 us
    ppermute x0 -> x3, starting transfers between devices: none -> 4.45 us  [per_device(): lax.ppermute(sent, 'expert', [(i, i ^ lap) for i in range(size)])]
    gather x8, local copies, waits for them, and re-layouts: 8.09 us -> 11.6 us  [spread_back(): compact_out[from_pos]]
    another operation x10 -> x9, local copies, waits for them, and re-layouts: 7.93 us -> 5.2 us
  transfers between devices with their start and end apart: 2 -> 5, of which waited for: 1 -> 3; matrix products, arithmetic and copies ran while one was open for 22% -> 23% of each run, Pallas kernels for 0% -> 0%
where the time goes in v1:
time: 284 us; the launch traced here: 280 us
  local copies, waits for them, and re-layouts  106 us (37%)
  matrix products  73.9 us (26%)
  other arithmetic  39.2 us (14%)
  waiting for transfers between devices  38.6 us (14%)
  starting transfers between devices  15.9 us (6%)
  between operations  6.01 us (2%)
    dot_general x13, matrix products, advance(): projected = jnp.dot(hidden, down_matrix, preferred_element_type=jnp.float32)  42 us
    dot_general x13, matrix products, advance(): jnp.dot(part_rows, gate_matrix, preferred_element_type=jnp.float32)  32 us
    ppermute x3, waiting for transfers between devices, per_device(): lax.ppermute(sent, 'expert', [(i, i ^ lap) for i in range(size)])  29.8 us
    gather x8, local copies, waits for them, and re-layouts, per_device(): recv_rows[member][gather_at]  20.7 us
    squeeze x1, local copies, waits for them, and re-layouts, per_device(): w_up[member]  17 us
    select_n x8, other arithmetic, per_device(): jnp.where(live_rows[:, None], recv_rows[member][gather_at], jnp.zeros((),...  14 us
    gather x8, local copies, waits for them, and re-layouts, spread_back(): compact_out[from_pos]  11.6 us
    gather x8, local copies, waits for them, and re-layouts, per_device(): recv_scale[member][gather_at]  9.86 us
  transfers between devices with their start and end apart: 5, of which 3 were waited for; matrix products, arithmetic and copies ran while one was open for 23% of the time, Pallas kernels for 0%

profile of v1, /device:TPU:0, one launch (start us, length us, event | category | flops | bytes accessed | tf_op | source)
XLA Modules:
  0.0 279.6 jit_solution(15443030918038372279)
XLA Ops:
  5.0 2.4 scatter_custom_fusion
  7.5 6.8 %gather_fusion = bf16[1024]{0:T(1024)(128)(2,1)S(1)} fusion(bf16[513]{0:T(1024)(128)(2,1)S(1)} %pad_maximum_fusion.1, s32[1024]{0:T(1024)S(1)} %get-tuple-element.570), kind=kCustom, calls=%fused_computation | custom fusion | bytes 8192 | tf_op jit(solution)/shard_map/gather | solution.py:103
  15.1 6.3 %all-to-all-start = ((bf16[4,2,128]{2,1,0:T(2,128)(2,1)}), bf16[4,2,128]{2,1,0:T(2,128)(2,1)S(1)}, u32[]{:S(2)}, u32[]{:S(2)}) async-start(bf16[4,2,128]{2,1,0:T(2,128)(2,1)} %reshape.1312), calls=%async_computation | async-start | bytes 4096 | tf_op jit(solution)/shard_map/all_to_all | solution.py:106
  21.4 9.6 %slice_bitcast_fusion = (bf16[768,1024]{1,0:T(8,128)(2,1)}, bf16[768,1024]{1,0:T(8,128)(2,1)}, bf16[768,1024]{1,0:T(8,128)(2,1)}, bf16[768,1024]{1,0:T(8,128)(2,...) fusion(bf16[8,768,1024]{2,1,0:T(8,128)(2,1)} %param.27), kind=kLoop, calls=%fused_computation.175 | loop fusion | bytes 25165824 | tf_op jit(solution)/shard_map/squeeze | solution.py:133
  31.0 17.0 %slice_bitcast_fusion.1 = (bf16[1024,768]{1,0:T(8,128)(2,1)S(1)}, bf16[1024,768]{1,0:T(8,128)(2,1)}, bf16[1024,768]{1,0:T(8,128)(2,1)}, bf16[1024,768]{1,0:T(8,1...) fusion(bf16[8,1024,768]{2,1,0:T(8,128)(2,1)} %param.26, ...), kind=kLoop, calls=%fused_computation.176 | loop fusion | bytes 50331648 | tf_op jit(solution)/shard_map/squeeze | solution.py:133
  48.1 5.4 %gather_fusion.2 = bf16[1024,1024]{1,0:T(8,128)(2,1)} fusion(bf16[65,1024]{1,0:T(8,128)(2,1)S(1)} %concatenate.8, s32[1024]{0:T(1024)S(1)} %get-tuple-element.569), kind=kCustom, calls=%fused_computation.2 | custom fusion | bytes 4198400 | tf_op jit(solution)/shard_map/gather | solution.py:102
  53.5 5.1 %all-to-all-start.1 = ((bf16[32,32,1024]{2,1,0:T(8,128)(2,1)}), bf16[32,32,1024]{2,1,0:T(8,128)(2,1)}, u32[]{:S(2)}, u32[]{:S(2)}) async-start(bf16[32,32,1024]{2,1,0:T(8,128)(2,1)} %bitcast.376), calls=%async_computation.1 | async-start | bytes 4194304 | tf_op jit(solution)/shard_map/all_to_all | solution.py:105
  97.5 8.9 %all-to-all-done.1 = bf16[32,32,1024]{2,1,0:T(8,128)(2,1)} async-done(((bf16[32,32,1024]{2,1,0:T(8,128)(2,1)}), bf16[32,32,1024]{2,1,0:T(8,128)(2,1)}, u32[]{:S(2)}, u32[]{:S(2)}) %all-to-all-start.1) | async-done | bytes 2097184 | tf_op jit(solution)/shard_map/all_to_all | solution.py:105
  106.4 1.8 copy.29
  109.4 2.7 gather_fusion.3
  112.2 1.8 broadcast_select_fusion.7
  114.7 12.1 %while.80 = (s32[]{:T(128)}, bf16[128,1024]{1,0:T(8,128)(2,1)}, s32[]{:T(128)}, bf16[128]{0:T(256)(128)(2,1)S(1)}, bf16[128,1024]{1,0:T(8,128)(2,1)}, /*index=5*...) while((s32[]{:T(128)}, bf16[128,1024]{1,0:T(8,128)(2,1)}, ...), condition=%wide.region_12.13_spmd, body=%wide.region_11.12_spmd.sunk | while | flops 302415936 | bytes 5506867 | solution.py:74
  114.7 2.5 fusion.291
  117.3 3.4 %fusion.292 = bf16[128,1024]{1,0:T(8,128)(2,1)} fusion(bf16[128,1024]{1,0:T(8,128)(2,1)} %get-tuple-element.1008, s32[]{:T(128)S(6)} %select_n.882, bf16[768,1024]{1,0:T(8,128)(2,1)} %get-tuple-element.1026, bf16[1024,768]{1,0:T(8,128)(2,1)} %get-tuple-element.1025, f32[64,768]{1,0:T(8,128)} %fusion.291, f32[64]{0:T(128)S(1)} %dynamic-slice_convert_fusion.16, ...), kind=kOutput, calls=%fused_computation.32.clone.1 | convolution fusion | flops 201752576 | bytes 3605760 | tf_op jit(solution)/shard_map/while/body/dot_general | solution.py:67
  120.7 2.5 fusion.291
  123.3 3.5 %fusion.292 = bf16[128,1024]{1,0:T(8,128)(2,1)} fusion(bf16[128,1024]{1,0:T(8,128)(2,1)} %get-tuple-element.1008, s32[]{:T(128)S(6)} %select_n.882, bf16[768,1024]{1,0:T(8,128)(2,1)} %get-tuple-element.1026, bf16[1024,768]{1,0:T(8,128)(2,1)} %get-tuple-element.1025, f32[64,768]{1,0:T(8,128)} %fusion.291, f32[64]{0:T(128)S(1)} %dynamic-slice_convert_fusion.16, ...), kind=kOutput, calls=%fused_computation.32.clone.1 | convolution fusion | flops 201752576 | bytes 3605760 | tf_op jit(solution)/shard_map/while/body/dot_general | solution.py:67
  126.8 2.7 gather_fusion.6
  129.5 1.7 broadcast_select_fusion.6
  132.0 6.1 %while.81 = (s32[]{:T(128)}, bf16[128,1024]{1,0:T(8,128)(2,1)}, s32[]{:T(128)}, bf16[128]{0:T(256)(128)(2,1)S(1)}, bf16[128,1024]{1,0:T(8,128)(2,1)}, /*index=5*...) while((s32[]{:T(128)}, bf16[128,1024]{1,0:T(8,128)(2,1)}, ...), condition=%wide.region_21.22_spmd, body=%wide.region_20.21_spmd.sunk | while | flops 302415936 | bytes 5506867 | solution.py:74
  132.0 2.6 fusion.298
  134.6 3.5 %fusion.299 = bf16[128,1024]{1,0:T(8,128)(2,1)} fusion(bf16[128,1024]{1,0:T(8,128)(2,1)} %get-tuple-element.1044, s32[]{:T(128)S(6)} %select_n.883, bf16[768,1024]{1,0:T(8,128)(2,1)} %get-tuple-element.1062, bf16[1024,768]{1,0:T(8,128)(2,1)} %get-tuple-element.1061, f32[64,768]{1,0:T(8,128)} %fusion.298, f32[64]{0:T(128)S(1)} %dynamic-slice_convert_fusion.17, ...), kind=kOutput, calls=%fused_computation.50.clone.1 | convolution fusion | flops 201752576 | bytes 3605760 | tf_op jit(solution)/shard_map/while/body/dot_general | solution.py:67
  138.1 2.7 gather_fusion.9
  140.8 1.8 broadcast_select_fusion.5
  143.3 6.1 %while.82 = (s32[]{:T(128)}, bf16[128,1024]{1,0:T(8,128)(2,1)}, s32[]{:T(128)}, bf16[128]{0:T(256)(128)(2,1)S(1)}, bf16[128,1024]{1,0:T(8,128)(2,1)}, /*index=5*...) while((s32[]{:T(128)}, bf16[128,1024]{1,0:T(8,128)(2,1)}, ...), condition=%wide.region_30.31_spmd, body=%wide.region_29.30_spmd.sunk | while | flops 302415936 | bytes 5506867 | solution.py:74
  143.3 2.5 fusion.305
  146.0 3.4 %fusion.306 = bf16[128,1024]{1,0:T(8,128)(2,1)} fusion(bf16[128,1024]{1,0:T(8,128)(2,1)} %get-tuple-element.1080, s32[]{:T(128)S(6)} %select_n.884, bf16[768,1024]{1,0:T(8,128)(2,1)} %get-tuple-element.1098, bf16[1024,768]{1,0:T(8,128)(2,1)} %get-tuple-element.1097, f32[64,768]{1,0:T(8,128)} %fusion.305, f32[64]{0:T(128)S(1)} %dynamic-slice_convert_fusion.18, ...), kind=kOutput, calls=%fused_computation.68.clone.1 | convolution fusion | flops 201752576 | bytes 3605760 | tf_op jit(solution)/shard_map/while/body/dot_general | solution.py:67
  149.4 2.7 gather_fusion.12
  152.2 1.8 broadcast_select_fusion.4
  154.7 12.1 %while.83 = (s32[]{:T(128)}, bf16[128,1024]{1,0:T(8,128)(2,1)}, s32[]{:T(128)}, bf16[128]{0:T(256)(128)(2,1)S(1)}, bf16[128,1024]{1,0:T(8,128)(2,1)}, /*index=5*...) while((s32[]{:T(128)}, bf16[128,1024]{1,0:T(8,128)(2,1)}, ...), condition=%wide.region_39.40_spmd, body=%wide.region_38.39_spmd.sunk | while | flops 302415936 | bytes 5506867 | solution.py:74
  154.7 2.5 fusion.312
  157.3 3.5 %fusion.313 = bf16[128,1024]{1,0:T(8,128)(2,1)} fusion(bf16[128,1024]{1,0:T(8,128)(2,1)} %get-tuple-element.1116, s32[]{:T(128)S(6)} %select_n.885, bf16[768,1024]{1,0:T(8,128)(2,1)} %get-tuple-element.1134, bf16[1024,768]{1,0:T(8,128)(2,1)} %get-tuple-element.1133, f32[64,768]{1,0:T(8,128)} %fusion.312, f32[64]{0:T(128)S(1)} %dynamic-slice_convert_fusion.19, ...), kind=kOutput, calls=%fused_computation.86.clone.1 | convolution fusion | flops 201752576 | bytes 3605760 | tf_op jit(solution)/shard_map/while/body/dot_general | solution.py:67
  160.7 2.5 fusion.312
  163.3 3.5 %fusion.313 = bf16[128,1024]{1,0:T(8,128)(2,1)} fusion(bf16[128,1024]{1,0:T(8,128)(2,1)} %get-tuple-element.1116, s32[]{:T(128)S(6)} %select_n.885, bf16[768,1024]{1,0:T(8,128)(2,1)} %get-tuple-element.1134, bf16[1024,768]{1,0:T(8,128)(2,1)} %get-tuple-element.1133, f32[64,768]{1,0:T(8,128)} %fusion.312, f32[64]{0:T(128)S(1)} %dynamic-slice_convert_fusion.19, ...), kind=kOutput, calls=%fused_computation.86.clone.1 | convolution fusion | flops 201752576 | bytes 3605760 | tf_op jit(solution)/shard_map/while/body/dot_general | solution.py:67
  166.8 2.7 gather_fusion.15
  169.5 1.8 broadcast_select_fusion.3
  172.0 6.1 %while.84 = (s32[]{:T(128)}, bf16[128,1024]{1,0:T(8,128)(2,1)}, s32[]{:T(128)}, bf16[128]{0:T(256)(128)(2,1)S(1)}, bf16[128,1024]{1,0:T(8,128)(2,1)}, /*index=5*...) while((s32[]{:T(128)}, bf16[128,1024]{1,0:T(8,128)(2,1)}, ...), condition=%wide.region_48.49_spmd, body=%wide.region_47.48_spmd.sunk | while | flops 302415936 | bytes 5506867 | solution.py:74
  172.0 2.5 fusion.319
  174.7 3.5 %fusion.320 = bf16[128,1024]{1,0:T(8,128)(2,1)} fusion(bf16[128,1024]{1,0:T(8,128)(2,1)} %get-tuple-element.1152, s32[]{:T(128)S(6)} %select_n.886, bf16[768,1024]{1,0:T(8,128)(2,1)} %get-tuple-element.1170, bf16[1024,768]{1,0:T(8,128)(2,1)} %get-tuple-element.1169, f32[64,768]{1,0:T(8,128)} %fusion.319, f32[64]{0:T(128)S(1)} %dynamic-slice_convert_fusion.20, ...), kind=kOutput, calls=%fused_computation.104.clone.1 | convolution fusion | flops 201752576 | bytes 3605760 | tf_op jit(solution)/shard_map/while/body/dot_general | solution.py:67
  178.1 2.7 gather_fusion.18
  180.8 1.7 broadcast_select_fusion.2
  183.3 12.2 %while.85 = (s32[]{:T(128)}, bf16[128,1024]{1,0:T(8,128)(2,1)}, s32[]{:T(128)}, bf16[128]{0:T(256)(128)(2,1)S(1)}, bf16[128,1024]{1,0:T(8,128)(2,1)}, /*index=5*...) while((s32[]{:T(128)}, bf16[128,1024]{1,0:T(8,128)(2,1)}, ...), condition=%wide.region_57.58_spmd, body=%wide.region_56.57_spmd.sunk | while | flops 302415936 | bytes 5506867 | solution.py:74
  183.3 2.6 fusion.326
  186.0 3.4 %fusion.327 = bf16[128,1024]{1,0:T(8,128)(2,1)} fusion(bf16[128,1024]{1,0:T(8,128)(2,1)} %get-tuple-element.1188, s32[]{:T(128)S(6)} %select_n.887, bf16[768,1024]{1,0:T(8,128)(2,1)} %get-tuple-element.1206, bf16[1024,768]{1,0:T(8,128)(2,1)} %get-tuple-element.1205, f32[64,768]{1,0:T(8,128)} %fusion.326, f32[64]{0:T(128)S(1)} %dynamic-slice_convert_fusion.21, ...), kind=kOutput, calls=%fused_computation.122.clone.1 | convolution fusion | flops 201752576 | bytes 3605760 | tf_op jit(solution)/shard_map/while/body/dot_general | solution.py:67
  189.4 2.6 fusion.326
  192.0 3.5 %fusion.327 = bf16[128,1024]{1,0:T(8,128)(2,1)} fusion(bf16[128,1024]{1,0:T(8,128)(2,1)} %get-tuple-element.1188, s32[]{:T(128)S(6)} %select_n.887, bf16[768,1024]{1,0:T(8,128)(2,1)} %get-tuple-element.1206, bf16[1024,768]{1,0:T(8,128)(2,1)} %get-tuple-element.1205, f32[64,768]{1,0:T(8,128)} %fusion.326, f32[64]{0:T(128)S(1)} %dynamic-slice_convert_fusion.21, ...), kind=kOutput, calls=%fused_computation.122.clone.1 | convolution fusion | flops 201752576 | bytes 3605760 | tf_op jit(solution)/shard_map/while/body/dot_general | solution.py:67
  195.5 2.7 gather_fusion.21
  198.2 1.7 broadcast_select_fusion.1
  200.7 11.3 %while.86 = (s32[]{:T(128)}, bf16[128,1024]{1,0:T(8,128)(2,1)}, s32[]{:T(128)}, bf16[128]{0:T(256)(128)(2,1)S(1)}, bf16[128,1024]{1,0:T(8,128)(2,1)}, /*index=5*...) while((s32[]{:T(128)}, bf16[128,1024]{1,0:T(8,128)(2,1)}, ...), condition=%wide.region_66.67_spmd, body=%wide.region_65.66_spmd.sunk | while | flops 302415936 | bytes 5506867 | solution.py:74
  200.7 2.5 fusion.333
  203.3 3.0 %fusion.334 = bf16[128,1024]{1,0:T(8,128)(2,1)} fusion(bf16[128,1024]{1,0:T(8,128)(2,1)} %get-tuple-element.1224, s32[]{:T(128)S(6)} %select_n.888, bf16[768,1024]{1,0:T(8,128)(2,1)} %get-tuple-element.1242, bf16[1024,768]{1,0:T(8,128)(2,1)S(1)} %get-tuple-element.1241, f32[64,768]{1,0:T(8,128)} %fusion.333, ...), kind=kOutput, calls=%fused_computation.140.clone.1 | convolution fusion | flops 201752576 | bytes 3605760 | tf_op jit(solution)/shard_map/while/body/dot_general | solution.py:67
  206.3 2.5 fusion.333
  209.0 3.1 %fusion.334 = bf16[128,1024]{1,0:T(8,128)(2,1)} fusion(bf16[128,1024]{1,0:T(8,128)(2,1)} %get-tuple-element.1224, s32[]{:T(128)S(6)} %select_n.888, bf16[768,1024]{1,0:T(8,128)(2,1)} %get-tuple-element.1242, bf16[1024,768]{1,0:T(8,128)(2,1)S(1)} %get-tuple-element.1241, f32[64,768]{1,0:T(8,128)} %fusion.333, ...), kind=kOutput, calls=%fused_computation.140.clone.1 | convolution fusion | flops 201752576 | bytes 3605760 | tf_op jit(solution)/shard_map/while/body/dot_general | solution.py:67
  213.6 1.7 broadcast_select_fusion
  215.3 9.2 %while.87 = (s32[]{:T(128)}, bf16[128,1024]{1,0:T(8,128)(2,1)S(1)}, s32[]{:T(128)}, bf16[128]{0:T(256)(128)(2,1)S(1)}, bf16[128,1024]{1,0:T(8,128)(2,1)}, /*inde...) while((s32[]{:T(128)}, bf16[128,1024]{1,0:T(8,128)(2,1)S(1)}, ...), condition=%wide.region_75.76_spmd, body=%wide.region_74.75_spmd.sunk | while | flops 302415936 | bytes 5507123 | solution.py:74
  215.4 2.0 fusion.340
  217.4 2.4 fusion.341
  219.9 2.0 fusion.340
  221.9 2.4 fusion.341
  224.6 2.1 gather_fusion.4
  239.5 3.0 %collective-permute-start = (bf16[8,32,1024]{2,1,0:T(8,128)(2,1)S(1)}, bf16[8,32,1024]{2,1,0:T(8,128)(2,1)S(1)}, u32[]{:S(2)}, u32[]{:S(2)}) collective-permute-start(bf16[8,32,1024]{2,1,0:T(8,128)(2,1)S(1)} %get-tuple-element.560), channel_id=1, source_target_pairs={{0,4},{4,0},{8,12},{12,8},{1,5},{5,1},{9,13},{13,9},{2,6},{6,2},{1... | collective-permute-start | bytes 1572872 | tf_op jit(solution)/shard_map/ppermute | solution.py:149
  242.5 12.2 %collective-permute-done.2 = bf16[8,32,1024]{2,1,0:T(8,128)(2,1)S(1)} collective-permute-done((bf16[8,32,1024]{2,1,0:T(8,128)(2,1)S(1)}, bf16[8,32,1024]{2,1,0:T(8,128)(2,1)S(1)}, u32[]{:S(2)}, u32[]{:S(2)}) %collective-permute-start.2) | collective-permute-done | bytes 524320 | tf_op jit(solution)/shard_map/ppermute | solution.py:149
  254.7 17.5 %collective-permute-done.1 = bf16[8,32,1024]{2,1,0:T(8,128)(2,1)S(1)} collective-permute-done((bf16[8,32,1024]{2,1,0:T(8,128)(2,1)S(1)}, bf16[8,32,1024]{2,1,0:T(8,128)(2,1)S(1)}, u32[]{:S(2)}, u32[]{:S(2)}) %collective-permute-start.1) | collective-permute-done | bytes 524320 | tf_op jit(solution)/shard_map/ppermute | solution.py:149
  273.9 2.3 gather_fusion.26
  276.1 2.1 gather_fusion.27
  (225 shorter events, 63.7 us)
Async XLA Ops:
  15.1 38.5 %all-to-all-start = ((bf16[4,2,128]{2,1,0:T(2,128)(2,1)}), bf16[4,2,128]{2,1,0:T(2,128)(2,1)S(1)}, u32[]{:S(2)}, u32[]{:S(2)}) async-start(bf16[4,2,128]{2,1,0:T(2,128)(2,1)} %reshape.1312), calls=%async_computation | async-start | bytes 4096 | tf_op jit(solution)/shard_map/all_to_all | solution.py:106
  31.0 17.1 %copy-start.12 = (bf16[64,1024]{1,0:T(8,128)(2,1)S(1)}, bf16[64,1024]{1,0:T(8,128)(2,1)}, u32[]{:S(2)}) copy-start(bf16[64,1024]{1,0:T(8,128)(2,1)} %param.22) | copy-start | bytes 393220
  53.5 52.8 %all-to-all-start.1 = ((bf16[32,32,1024]{2,1,0:T(8,128)(2,1)}), bf16[32,32,1024]{2,1,0:T(8,128)(2,1)}, u32[]{:S(2)}, u32[]{:S(2)}) async-start(bf16[32,32,1024]{2,1,0:T(8,128)(2,1)} %bitcast.376), calls=%async_computation.1 | async-start | bytes 4194304 | tf_op jit(solution)/shard_map/all_to_all | solution.py:105
  138.1 5.2 %copy-start.17 = (bf16[128]{0:T(256)(128)(2,1)S(1)}, bf16[128]{0:T(256)(128)(2,1)}, u32[]{:S(2)}) copy-start(bf16[128]{0:T(256)(128)(2,1)} %broadcast_select_fusion.13) | copy-start | bytes 772
  149.4 5.2 %copy-start.16 = (bf16[128]{0:T(256)(128)(2,1)S(1)}, bf16[128]{0:T(256)(128)(2,1)}, u32[]{:S(2)}) copy-start(bf16[128]{0:T(256)(128)(2,1)} %broadcast_select_fusion.12) | copy-start | bytes 772
  166.8 5.2 %copy-start.15 = (bf16[128]{0:T(256)(128)(2,1)S(1)}, bf16[128]{0:T(256)(128)(2,1)}, u32[]{:S(2)}) copy-start(bf16[128]{0:T(256)(128)(2,1)} %broadcast_select_fusion.11) | copy-start | bytes 772
  178.1 5.2 %copy-start.14 = (bf16[128]{0:T(256)(128)(2,1)S(1)}, bf16[128]{0:T(256)(128)(2,1)}, u32[]{:S(2)}) copy-start(bf16[128]{0:T(256)(128)(2,1)} %broadcast_select_fusion.10) | copy-start | bytes 772
  195.5 5.2 %copy-start.13 = (bf16[128]{0:T(256)(128)(2,1)S(1)}, bf16[128]{0:T(256)(128)(2,1)}, u32[]{:S(2)}) copy-start(bf16[128]{0:T(256)(128)(2,1)} %broadcast_select_fusion.9) | copy-start | bytes 772
  212.0 3.3 %copy-start = (bf16[1024,768]{1,0:T(8,128)(2,1)S(1)}, bf16[1024,768]{1,0:T(8,128)(2,1)}, u32[]{:S(2)}) copy-start(bf16[1024,768]{1,0:T(8,128)(2,1)} %get-tuple-element.1252) | copy-start | bytes 4718596
  224.5 2.2 copy-start.1
  226.6 1.0 copy-start.2
  227.6 1.0 copy-start.3
  228.5 1.6 copy-start.4
  230.1 1.6 copy-start.5
  231.7 1.6 copy-start.6
  234.8 1.8 copy-start.7
  234.8 2.0 copy-start.8
  236.4 0.9 copy-start.9
  236.4 1.1 copy-start.10
  236.4 1.2 copy-start.11
  238.0 16.7 %collective-permute-start.2 = (bf16[8,32,1024]{2,1,0:T(8,128)(2,1)S(1)}, bf16[8,32,1024]{2,1,0:T(8,128)(2,1)S(1)}, u32[]{:S(2)}, u32[]{:S(2)}) collective-permute-start(bf16[8,32,1024]{2,1,0:T(8,128)(2,1)S(1)} %get-tuple-element.558), channel_id=1, source_target_pairs={{0,12},{4,8},{8,4},{12,0},{1,13},{5,9},{9,5},{13,1},{2,14},{6,10},... | collective-permute-start | bytes 1572872 | tf_op jit(solution)/shard_map/ppermute | solution.py:149
  239.5 32.7 %collective-permute-start.1 = (bf16[8,32,1024]{2,1,0:T(8,128)(2,1)S(1)}, bf16[8,32,1024]{2,1,0:T(8,128)(2,1)S(1)}, u32[]{:S(2)}, u32[]{:S(2)}) collective-permute-start(bf16[8,32,1024]{2,1,0:T(8,128)(2,1)S(1)} %get-tuple-element.559), channel_id=1, source_target_pairs={{0,8},{4,12},{8,0},{12,4},{1,9},{5,13},{9,1},{13,5},{2,10},{6,14},... | collective-permute-start | bytes 1572872 | tf_op jit(solution)/shard_map/ppermute | solution.py:149
  239.5 32.7 %collective-permute-start = (bf16[8,32,1024]{2,1,0:T(8,128)(2,1)S(1)}, bf16[8,32,1024]{2,1,0:T(8,128)(2,1)S(1)}, u32[]{:S(2)}, u32[]{:S(2)}) collective-permute-start(bf16[8,32,1024]{2,1,0:T(8,128)(2,1)S(1)} %get-tuple-element.560), channel_id=1, source_target_pairs={{0,4},{4,0},{8,12},{12,8},{1,5},{5,1},{9,13},{13,9},{2,6},{6,2},{1... | collective-permute-start | bytes 1572872 | tf_op jit(solution)/shard_map/ppermute | solution.py:149
